TPU v7x, 256 devices: a whole 4x4x8 slice. The times are simulated.
256 devices in a mesh: tm: 16 (over z, core), space: 16 (over x, y).
Axes of the slice: x: 4, y: 4, z: 8, core: 2. Of those that a mesh axis runs over, the one named last changes fastest.
Arguments:
- concentration: float32 [4, 16, 1024, 2048], P(None, 'tm', 'space'), may hold values from -5.5 to 5.5
- forcing: float32 [4, 16, 1024, 2048], P(None, 'tm', 'space'), may hold values from -5.5 to 5.5
- eigenbasis: bfloat16 [2048, 2048], replicated, may hold values from -0.125 to 0.125
- eigenvalues: float32 [2048], replicated, may hold values from -0.5 to -0.001, as said below
- settle_table: float32 [8], replicated, may hold values from 0.002 to 0.5, as said below
- fraction_class: int32 [4], replicated, may hold values from 0 to 7
- bed_mask: int32 [1024, 2048], P('space'), may hold values 0 or 1
Outputs:
- updated: float32 [4, 16, 1024, 2048], P(None, 'tm', 'space')
Inputs may be any that keep to these rules, and one draw needn't show every extreme that they name: `fraction_class`: index into settle_table. `bed_mask`: 1 marks a bed cell. `eigenvalues`: negative. `settle_table`: positive.
All inputs are finite; a program needn't handle non-finite values. No bound on the sum of `bed_mask` on one device may be relied on, other than what follows from the above.
Results may differ from a plain program's by a relative error of at most 0.0055.
Values may be sent and summed in bfloat16 or wider, within the bound.
A program may use at most 64 MiB of HBM per device.

v0:
```python
import math
import jax
import jax.numpy as jnp
from jax import lax
from jax.sharding import PartitionSpec as P

CIRCULANT_ALPHA = 0.5
VERTICAL_DIFFUSION = 0.06
DEPOSITION = 0.1


def extended(block, sides, width):
    for axis, dim in sides:
        count = lax.axis_size(axis)
        forward = [(i, i + 1) for i in range(count - 1)]
        backward = [(target, source) for source, target in forward]
        low = lax.ppermute(
            lax.slice_in_dim(block, block.shape[dim] - width, None, axis=dim), axis, forward
        )
        high = lax.ppermute(lax.slice_in_dim(block, 0, width, axis=dim), axis, backward)
        block = jnp.concatenate([low, block, high], axis=dim)
    return block


def from_behind(value, axis, steps):
    count = lax.axis_size(axis)
    initial, last = (max(0, -steps), min(count, count - steps))
    return lax.ppermute(value, axis, [(source, source + steps) for source in range(initial, last)])


def twiddles(first_index, second_index, length):
    products = first_index[:, None] * second_index[None, :] % length
    angle_grid = 2.0 * math.pi / length * products.astype(jnp.float32)
    return (jnp.cos(angle_grid), jnp.sin(angle_grid))


def apply_table(table, values):
    return jnp.einsum(
        "kn,fnrx->fkrx", table, values.astype(jnp.float32), precision=lax.Precision.HIGHEST
    )


def to_space(modal, eigenbasis):
    return lax.dot_general(
        modal, eigenbasis, (((1,), (1,)), ((), ())), preferred_element_type=jnp.float32
    )


def solve_shifted(
    real_part, imag_part, freq_index, length, decay_ratio, eigenbasis, eigenvalues, diagonal
):
    layout = real_part.shape
    columns = layout[-1]
    stacked = (
        jnp.concatenate([real_part, imag_part], axis=0).astype(jnp.bfloat16).reshape(-1, columns)
    )
    modal = jnp.dot(stacked, eigenbasis, preferred_element_type=jnp.float32).reshape((2,) + layout)
    angles = 2.0 * math.pi / length * freq_index.astype(jnp.float32)
    shift_real = (
        (1.0 - decay_ratio * jnp.cos(angles))[None, :, None, None]
        - eigenvalues[None, None, None, :]
        + diagonal[:, None, None, None]
    )
    shift_imag = (decay_ratio * jnp.sin(angles))[None, :, None, None]
    magnitude = shift_real * shift_real + shift_imag * shift_imag
    scaled_real = (modal[0] * shift_real + modal[1] * shift_imag) / magnitude
    scaled_imag = (modal[1] * shift_real - modal[0] * shift_imag) / magnitude
    scaled = (
        jnp.concatenate([scaled_real, scaled_imag], axis=0)
        .astype(jnp.bfloat16)
        .reshape(-1, columns)
    )
    back = to_space(scaled, eigenbasis).astype(jnp.bfloat16).reshape((2,) + layout)
    return (back[0], back[1])


def on_device(
    concentration, forcing, eigenbasis, eigenvalues, settle_table, fraction_class, bed_mask
):
    fractions, slices, row_count, columns = concentration.shape
    tm_devices = lax.axis_size("tm")
    length = slices * tm_devices
    classes = settle_table.shape[0]
    onehot = (fraction_class[:, None] == jnp.arange(classes, dtype=jnp.int32)[None, :]).astype(
        jnp.float32
    )
    settling = jnp.sum(onehot * settle_table[None, :], axis=1)
    diagonal = 2.0 * VERTICAL_DIFFUSION + settling
    decay_ratio = CIRCULANT_ALPHA ** (1.0 / length)
    first_slice = lax.axis_index("tm") * slices
    slice_index = first_slice + jnp.arange(slices, dtype=jnp.int32)
    slice_times = slice_index.astype(jnp.float32)
    scale_up = decay_ratio**slice_times
    scale_down = decay_ratio ** (-slice_times)
    bed_cells = bed_mask.astype(jnp.float32)
    padded = extended(concentration, (("space", 2),), 1)
    upper_row = padded[:, :, :-2]
    lower_row = padded[:, :, 2:]
    vertical = (
        VERTICAL_DIFFUSION * (lower_row - 2.0 * concentration + upper_row)
        + settling[:, None, None, None] * (upper_row - concentration)
        - DEPOSITION * bed_cells[None, None] * concentration
    )
    coupled = (
        jnp.dot(
            concentration.astype(jnp.bfloat16).reshape(-1, columns),
            eigenbasis,
            preferred_element_type=jnp.float32,
        )
        * eigenvalues[None, :]
    ).astype(jnp.bfloat16)
    along_x = to_space(coupled, eigenbasis).reshape(concentration.shape)
    last_slice = from_behind(concentration, "tm", 1)
    earlier = jnp.concatenate([last_slice, concentration[:, : slices - 1]], axis=1)
    residual = forcing - (concentration - along_x - vertical - earlier)
    scaled = (scale_up[None, :, None, None] * residual).astype(jnp.bfloat16)
    by_rows = lax.all_to_all(scaled, "tm", split_axis=2, concat_axis=1, tiled=True)
    all_index = jnp.arange(length, dtype=jnp.int32)
    cosine_table, sine_table = twiddles(all_index, all_index, length)
    real_part = apply_table(cosine_table, by_rows)
    imag_part = -apply_table(sine_table, by_rows)
    back_real, back_imag = solve_shifted(
        real_part, imag_part, all_index, length, decay_ratio, eigenbasis, eigenvalues, diagonal
    )
    relaxed_rows = (
        apply_table(cosine_table, back_real) - apply_table(sine_table, back_imag)
    ) / length
    relaxed = lax.all_to_all(relaxed_rows, "tm", split_axis=1, concat_axis=2, tiled=True)
    return concentration + scale_down[None, :, None, None] * relaxed


def solution(mesh):
    return jax.shard_map(
        on_device,
        mesh=mesh,
        in_specs=(
            P(None, "tm", "space", None),
            P(None, "tm", "space", None),
            P(),
            P(),
            P(),
            P(),
            P("space", None),
        ),
        out_specs=P(None, "tm", "space", None),
        check_vma=False,
    )
```

profile of v0, /device:TPU:1, one launch (start us, length us, event | category | flops | bytes accessed | tf_op | source)
XLA Modules:
  0.0 189.0 jit_solution(3372452159803485570)
XLA Ops:
  0.0 0.0 copy-start.3
  0.0 5.0 %collective-permute-start.2 = (f32[4,1,64,2048]{3,2,1,0:T(8,128)}, f32[4,1,64,2048]{3,2,1,0:T(8,128)}, u32[]{:S(2)}, u32[]{:S(2)}) collective-permute-start(f32[4,1,64,2048]{3,2,1,0:T(8,128)} %param.7), channel_id=1, source_target_pairs={{0,16},{16,32},{32,48},{48,64},{64,80},{80,96},{96,112},{112,128},... | collective-permute-start | bytes 6291464 | tf_op jit(solution)/shard_map/ppermute | solution.py:28
  5.1 1.1 fusion.61
  6.1 1.3 collective-permute-start
  7.4 0.0 copy-start.4
  7.5 4.0 %collective-permute-start.1 = (f32[4,1,1,2048]{3,2,1,0:T(1,128)S(1)}, f32[4,1,1,2048]{3,2,1,0:T(1,128)S(1)}, u32[]{:S(2)}, u32[]{:S(2)}) collective-permute-start(f32[4,1,1,2048]{3,2,1,0:T(1,128)S(1)} %get-tuple-element.12), channel_id=1, source_target_pairs={{0,1},{1,2},{2,3},{3,4},{4,5},{5,6},{6,7},{7,8},{8,9},{9,10},{10,1... | collective-permute-start | bytes 98312 | tf_op jit(solution)/shard_map/ppermute | solution.py:17
  11.4 2.7 %convert_element_type.63 = bf16[4,1,64,2048]{3,2,1,0:T(8,128)(2,1)} convert(f32[4,1,64,2048]{3,2,1,0:T(8,128)} %param.7) | non-fusion elementwise | flops 524288 | bytes 3145728 | tf_op jit(solution)/shard_map/convert_element_type | solution.py:106
  14.2 0.0 copy-done.3
  14.2 0.0 copy-done.4
  14.2 0.0 copy-start.5
  14.2 0.0 copy-start.6
  14.2 0.0 copy-start
  14.3 12.0 %fusion.25 = f32[256,2048]{1,0:T(8,128)} fusion(bf16[2048,2048]{1,0:T(8,128)(2,1)} %param.9, bf16[256,2048]{1,0:T(8,128)(2,1)} %bitcast.37, f32[2048]{0:T(1024)S(1)} %copy-done.4), kind=kOutput, calls=%fused_computation.38 | convolution fusion | flops 4296015872 | bytes 11542528 | tf_op jit(solution)/shard_map/dot_general | solution.py:44
  26.3 0.0 copy-done.5
  26.3 0.0 copy-done.6
  26.3 0.2 select_reduce_fusion
  26.5 0.0 collective-permute-done
  26.6 0.0 collective-permute-done.1
  26.6 1.8 collective-permute-done.2
  28.3 0.0 copy-done
  28.3 3.5 %fusion.15 = bf16[4,1,64,2048]{3,2,1,0:T(8,128)(2,1)S(1)} fusion(f32[4,1,64,2048]{3,2,1,0:T(8,128)} %param.8, f32[4,1,64,2048]{3,2,1,0:T(8,128)} %collective-permute-done.2, f32[4,1,64,2048]{3,2,1,0:T(8,128)S(1)} %copy-done, f32[4,1,1,2048]{3,2,1,0:T(1,128)S(1)} %collective-permute-done.1, f32[4,1,1,2048]{3,2,1,0:T(1,128)S(1)} %collective-permute-done, ...), kind=kLoop, calls=%fused_computation.21 | loop fusion | flops 8912896 | bytes 10027028 | tf_op jit(solution)/shard_map/convert_element_type | solution.py:116
  31.9 1.8 copy.66
  33.7 10.6 %all-to-all-start = ((bf16[4,1,64,2048]{3,0,1,2:T(4,128)(2,1)}), bf16[4,1,64,2048]{3,0,1,2:T(4,128)(2,1)S(1)}, u32[]{:S(2)}, u32[]{:S(2)}) async-start(bf16[4,1,64,2048]{3,0,1,2:T(4,128)(2,1)} %copy.66), calls=%async_computation | async-start | bytes 2097152 | tf_op jit(solution)/shard_map/all_to_all | solution.py:117
  44.5 0.1 broadcast_subtract_fusion
  44.6 1.2 broadcast_add_fusion
  45.7 26.6 %all-to-all-done = bf16[4,1,64,2048]{3,0,1,2:T(4,128)(2,1)S(1)} async-done(((bf16[4,1,64,2048]{3,0,1,2:T(4,128)(2,1)}), bf16[4,1,64,2048]{3,0,1,2:T(4,128)(2,1)S(1)}, u32[]{:S(2)}, u32[]{:S(2)}) %all-to-all-start) | async-done | bytes 1048608 | tf_op jit(solution)/shard_map/all_to_all | solution.py:117
  72.3 1.6 fusion.4
  73.9 1.6 fusion.5
  75.6 0.2 pad_maximum_fusion.2
  75.8 3.0 %copy.69 = bf16[8,16,4,2048]{3,2,1,0:T(4,128)(2,1)} copy(bf16[8,16,4,2048]{3,1,2,0:T(8,128)(2,1)S(1)} %pad_maximum_fusion.2) | data formatting | bytes 4194304 | tf_op jit(solution)/shard_map/concatenate | solution.py:55
  78.7 4.0 %convert_element_type.68 = bf16[512,2048]{1,0:T(8,128)(2,1)} reshape(bf16[8,16,4,2048]{3,2,1,0:T(4,128)(2,1)} %copy.69) | data formatting | bytes 4194304 | tf_op jit(solution)/shard_map/convert_element_type | solution.py:55
  82.7 7.6 %fusion.62 = f32[512,2048]{1,0:T(8,128)S(1)} fusion(bf16[512,2048]{1,0:T(8,128)(2,1)} %convert_element_type.68, bf16[2048,2048]{1,0:T(8,128)(2,1)} %param.9), kind=kOutput, calls=%fused_computation.84 | convolution fusion | flops 4294967296 | bytes 14680064 | tf_op jit(solution)/shard_map/dot_general | solution.py:57
  90.3 2.3 %fusion.59 = (f32[256,2048]{1,0:T(8,128)}, f32[256,2048]{1,0:T(8,128)}) fusion(f32[512,2048]{1,0:T(8,128)S(1)} %fusion.62), kind=kLoop, calls=%fused_computation.81 | loop fusion | bytes 8388608 | tf_op jit(solution)/shard_map/slice | solution.py:66
  92.6 2.9 %squeeze.14 = f32[4,16,4,2048]{3,2,1,0:T(4,128)} reshape(f32[256,2048]{1,0:T(8,128)} %get-tuple-element.8) | data formatting | bytes 4194304 | tf_op jit(solution)/shard_map/squeeze | solution.py:66
  95.4 0.0 copy-start.1
  95.4 0.0 copy-start.2
  95.4 2.9 %squeeze.15 = f32[4,16,4,2048]{3,2,1,0:T(4,128)} reshape(f32[256,2048]{1,0:T(8,128)} %get-tuple-element.7) | data formatting | bytes 4194304 | tf_op jit(solution)/shard_map/squeeze | solution.py:66
  98.4 0.0 copy-done.1
  98.4 0.0 copy-done.2
  98.4 3.3 %fusion.18 = (bf16[4,16,4,2048]{3,2,1,0:T(4,128)(2,1)S(1)}, bf16[4,16,4,2048]{3,2,1,0:T(4,128)(2,1)S(1)}) fusion(f32[4,16,4,2048]{3,2,1,0:T(4,128)} %squeeze.15, f32[4,16,4,2048]{3,2,1,0:T(4,128)} %squeeze.14, f32[4,16,2048]{2,1,0:T(8,128)S(1)} %copy-done.2, f32[16]{0:T(128)S(1)} %sine_multiply_fusion, f32[4,16,2048]{2,1,0:T(8,128)S(1)} %copy-done.1), kind=kLoop, calls=%fused_computation.31 | loop fusion | flops 5242880 | bytes 7340096 | tf_op jit(solution)/shard_map/convert
  101.7 2.7 %pad_maximum_fusion.3 = bf16[8,16,4,2048]{3,2,1,0:T(4,128)(2,1)} fusion(bf16[4,16,4,2048]{3,2,1,0:T(4,128)(2,1)S(1)} %get-tuple-element.6, bf16[4,16,4,2048]{3,2,1,0:T(4,128)(2,1)S(1)} %get-tuple-element.5), kind=kLoop, calls=%fused_computation.26 | loop fusion | flops 1048576 | bytes 4194304 | tf_op jit(solution)/shard_map/concatenate | solution.py:69
  104.4 4.0 %convert_element_type.70 = bf16[512,2048]{1,0:T(8,128)(2,1)} reshape(bf16[8,16,4,2048]{3,2,1,0:T(4,128)(2,1)} %pad_maximum_fusion.3) | data formatting | bytes 4194304 | tf_op jit(solution)/shard_map/convert_element_type | solution.py:70
  108.3 8.5 %convolution_convert_fusion = bf16[512,2048]{1,0:T(8,128)(2,1)S(1)} fusion(bf16[512,2048]{1,0:T(8,128)(2,1)} %convert_element_type.70, bf16[2048,2048]{1,0:T(8,128)(2,1)} %param.9), kind=kOutput, calls=%fused_computation | convolution fusion | flops 4296015872 | bytes 12582912 | tf_op jit(solution)/shard_map/dot_general | solution.py:44
  116.9 1.5 fusion.60
  118.3 1.5 squeeze.16
  119.8 2.7 %fusion.21 = f32[4,4,2048,16]{2,3,1,0:T(8,128)} fusion(bf16[4,16,4,2048]{3,2,1,0:T(4,128)(2,1)S(1)} %squeeze.16), kind=kOutput, calls=%fused_computation.34 | convolution fusion | flops 100666880 | bytes 3145728 | tf_op jit(solution)/shard_map/kn,fnrx->fkrx/dot_general | solution.py:38
  122.5 1.5 squeeze.17
  123.9 3.1 %fusion.1 = f32[4,16,4,2048]{3,1,2,0:T(8,128)S(1)} fusion(f32[4,4,2048,16]{2,3,1,0:T(8,128)} %fusion.21, bf16[4,16,4,2048]{3,2,1,0:T(4,128)(2,1)S(1)} %squeeze.17), kind=kOutput, calls=%fused_computation.5 | convolution fusion | flops 101715456 | bytes 5242880 | tf_op jit(solution)/shard_map/kn,fnrx->fkrx/dot_general | solution.py:38
  127.0 2.7 %copy.72 = f32[4,16,4,2048]{3,2,0,1:T(4,128)} copy(f32[4,16,4,2048]{3,1,2,0:T(8,128)S(1)} %fusion.1) | data formatting | bytes 4194304 | tf_op jit(solution)/shard_map/div | solution.py:125
  129.7 4.6 %all-to-all-start.1 = ((f32[4,16,4,2048]{3,2,0,1:T(4,128)}), f32[4,16,4,2048]{3,2,0,1:T(4,128)}, u32[]{:S(2)}, u32[]{:S(2)}) async-start(f32[4,16,4,2048]{3,2,0,1:T(4,128)} %copy.72), calls=%async_computation.1 | async-start | bytes 4194304 | tf_op jit(solution)/shard_map/all_to_all | solution.py:128
  134.3 47.9 %all-to-all-done.1 = f32[4,16,4,2048]{3,2,0,1:T(4,128)} async-done(((f32[4,16,4,2048]{3,2,0,1:T(4,128)}), f32[4,16,4,2048]{3,2,0,1:T(4,128)}, u32[]{:S(2)}, u32[]{:S(2)}) %all-to-all-start.1) | async-done | bytes 2097184 | tf_op jit(solution)/shard_map/all_to_all | solution.py:128
  182.2 2.8 %copy_multiply_fusion = f32[4,16,4,2048]{3,1,2,0:T(8,128)S(1)} fusion(f32[4,16,4,2048]{3,2,0,1:T(4,128)} %all-to-all-done.1, f32[]{:T(128)S(6)} %pow.8), kind=kLoop, calls=%fused_computation.28 | loop fusion | flops 524288 | bytes 4194308 | tf_op jit(solution)/shard_map/mul | solution.py:129
  185.0 1.4 copy.74
  186.4 2.6 %copy_add_fusion = f32[4,1,64,2048]{3,2,1,0:T(8,128)} fusion(f32[4,1,64,2048]{3,2,1,0:T(8,128)S(1)} %copy-done, f32[4,1,64,2048]{3,0,2,1:T(4,128)S(1)} %bitcast.35), kind=kLoop, calls=%fused_computation.27 | loop fusion | flops 524288 | bytes 6291456 | tf_op jit(solution)/shard_map/add | solution.py:129
  (5 shorter events, 0.2 us)
Async XLA Ops:
  0.0 14.2 %copy-start.3 = (s32[64,2048]{1,0:T(8,128)S(1)}, s32[64,2048]{1,0:T(8,128)}, u32[]{:S(2)}) copy-start(s32[64,2048]{1,0:T(8,128)} %param.13) | copy-start | bytes 1572868
  0.0 28.3 %collective-permute-start.2 = (f32[4,1,64,2048]{3,2,1,0:T(8,128)}, f32[4,1,64,2048]{3,2,1,0:T(8,128)}, u32[]{:S(2)}, u32[]{:S(2)}) collective-permute-start(f32[4,1,64,2048]{3,2,1,0:T(8,128)} %param.7), channel_id=1, source_target_pairs={{0,16},{16,32},{32,48},{48,64},{64,80},{80,96},{96,112},{112,128},... | collective-permute-start | bytes 6291464 | tf_op jit(solution)/shard_map/ppermute | solution.py:28
  6.1 20.4 %collective-permute-start = (f32[4,1,1,2048]{3,2,1,0:T(1,128)S(1)}, f32[4,1,1,2048]{3,2,1,0:T(1,128)S(1)}, u32[]{:S(2)}, u32[]{:S(2)}) collective-permute-start(f32[4,1,1,2048]{3,2,1,0:T(1,128)S(1)} %get-tuple-element.11), channel_id=1, source_target_pairs={{1,0},{2,1},{3,2},{4,3},{5,4},{6,5},{7,6},{8,7},{9,8},{10,9},{11,1... | collective-permute-start | bytes 98312 | tf_op jit(solution)/shard_map/ppermute | solution.py:20
  7.4 6.8 %copy-start.4 = (f32[2048]{0:T(1024)S(1)}, f32[2048]{0:T(1024)}, u32[]{:S(2)}) copy-start(f32[2048]{0:T(1024)} %param.10) | copy-start | bytes 24580
  7.5 19.1 %collective-permute-start.1 = (f32[4,1,1,2048]{3,2,1,0:T(1,128)S(1)}, f32[4,1,1,2048]{3,2,1,0:T(1,128)S(1)}, u32[]{:S(2)}, u32[]{:S(2)}) collective-permute-start(f32[4,1,1,2048]{3,2,1,0:T(1,128)S(1)} %get-tuple-element.12), channel_id=1, source_target_pairs={{0,1},{1,2},{2,3},{3,4},{4,5},{5,6},{6,7},{7,8},{8,9},{9,10},{10,1... | collective-permute-start | bytes 98312 | tf_op jit(solution)/shard_map/ppermute | solution.py:17
  14.2 12.1 %copy-start.5 = (f32[8]{0:T(128)S(1)}, f32[8]{0:T(128)}, u32[]{:S(2)}) copy-start(f32[8]{0:T(128)} %param.11) | copy-start | bytes 100
  14.2 12.1 %copy-start.6 = (s32[4]{0:T(128)S(1)}, s32[4]{0:T(128)}, u32[]{:S(2)}) copy-start(s32[4]{0:T(128)} %param.12) | copy-start | bytes 52
  14.2 14.1 %copy-start = (f32[4,1,64,2048]{3,2,1,0:T(8,128)S(1)}, f32[4,1,64,2048]{3,2,1,0:T(8,128)}, u32[]{:S(2)}) copy-start(f32[4,1,64,2048]{3,2,1,0:T(8,128)} %param.7) | copy-start | bytes 6291460
  33.7 38.6 %all-to-all-start = ((bf16[4,1,64,2048]{3,0,1,2:T(4,128)(2,1)}), bf16[4,1,64,2048]{3,0,1,2:T(4,128)(2,1)S(1)}, u32[]{:S(2)}, u32[]{:S(2)}) async-start(bf16[4,1,64,2048]{3,0,1,2:T(4,128)(2,1)} %copy.66), calls=%async_computation | async-start | bytes 2097152 | tf_op jit(solution)/shard_map/all_to_all | solution.py:117
  95.4 3.0 %copy-start.1 = (f32[4,16,2048]{2,1,0:T(8,128)S(1)}, f32[4,16,2048]{2,1,0:T(8,128)}, u32[]{:S(2)}) copy-start(f32[4,16,2048]{2,1,0:T(8,128)} %get-tuple-element.13) | copy-start | bytes 1572868
  95.4 3.0 %copy-start.2 = (f32[4,16,2048]{2,1,0:T(8,128)S(1)}, f32[4,16,2048]{2,1,0:T(8,128)}, u32[]{:S(2)}) copy-start(f32[4,16,2048]{2,1,0:T(8,128)} %get-tuple-element.14) | copy-start | bytes 1572868
  129.7 52.5 %all-to-all-start.1 = ((f32[4,16,4,2048]{3,2,0,1:T(4,128)}), f32[4,16,4,2048]{3,2,0,1:T(4,128)}, u32[]{:S(2)}, u32[]{:S(2)}) async-start(f32[4,16,4,2048]{3,2,0,1:T(4,128)} %copy.72), calls=%async_computation.1 | async-start | bytes 4194304 | tf_op jit(solution)/shard_map/all_to_all | solution.py:128
where the time goes:
time: 190 us; the launch traced here: 189 us
  waiting for transfers between devices  76.3 us (40%)
  matrix products  37.2 us (20%)
  local copies, waits for them, and re-layouts  30.3 us (16%)
  starting transfers between devices  25.6 us (13%)
  other arithmetic  19.5 us (10%)
    all_to_all x1, waiting for transfers between devices, on_device(): lax.all_to_all(relaxed_rows, 'tm', split_axis=1, concat_axis=2, tiled=True)  47.9 us
    all_to_all x1, waiting for transfers between devices, on_device(): lax.all_to_all(scaled, 'tm', split_axis=2, concat_axis=1, tiled=True)  26.6 us
    dot_general x2, matrix products, to_space(): lax.dot_general(modal, eigenbasis, (((1,), (1,)), ((), ())), preferred_el...  20.6 us
    all_to_all x1, starting transfers between devices, on_device(): lax.all_to_all(scaled, 'tm', split_axis=2, concat_axis=1, tiled=True)  10.6 us
    dot_general x4, matrix products, apply_table(): jnp.einsum('kn,fnrx->fkrx', table, values.astype(jnp.float32), precision=...  9.01 us
    dot_general x1, matrix products, solve_shifted(): jnp.dot(stacked, eigenbasis, preferred_element_type=jnp.float32)  7.56 us
    squeeze x2, local copies, waits for them, and re-layouts, solve_shifted(): scaled_real = (modal[0] * shift_real + modal[1] * shift_imag) / magnitude  5.81 us
    ppermute x1, starting transfers between devices, from_behind(): lax.ppermute(value, axis, [(source, source + steps) for source in range(i...  5.05 us
  transfers between devices with their start and end apart: 5, of which 3 were waited for; matrix products, arithmetic and copies ran while one was open for 9% of the time, Pallas kernels for 0%

commit v1 on v0

--- a/solution.py
+++ b/solution.py
@@ -7,6 +7,12 @@
 CIRCULANT_ALPHA = 0.5
 VERTICAL_DIFFUSION = 0.06
 DEPOSITION = 0.1
+
+
+def stacked_exchange(block, axis, split, join):
+    pieces = jnp.split(block, lax.axis_size(axis), axis=split)
+    received = lax.all_to_all(jnp.stack(pieces), axis, 0, 0)
+    return jnp.concatenate(received, axis=join)
 
 
 def extended(block, sides, width):
@@ -114,7 +120,7 @@
     earlier = jnp.concatenate([last_slice, concentration[:, : slices - 1]], axis=1)
     residual = forcing - (concentration - along_x - vertical - earlier)
     scaled = (scale_up[None, :, None, None] * residual).astype(jnp.bfloat16)
-    by_rows = lax.all_to_all(scaled, "tm", split_axis=2, concat_axis=1, tiled=True)
+    by_rows = stacked_exchange(scaled, "tm", 2, 1)
     all_index = jnp.arange(length, dtype=jnp.int32)
     cosine_table, sine_table = twiddles(all_index, all_index, length)
     real_part = apply_table(cosine_table, by_rows)

time: 190 us -> 198 us (1.042)
  local copies, waits for them, and re-layouts: 30.3 us -> 39 us
    unnamed x14 -> x29, local copies, waits for them, and re-layouts: 0.04 us -> 9.88 us
where the time goes in v1:
time: 198 us; the launch traced here: 197 us
  waiting for transfers between devices  76.3 us (39%)
  local copies, waits for them, and re-layouts  39 us (20%)
  matrix products  36.5 us (18%)
  starting transfers between devices  25.6 us (13%)
  other arithmetic  19.5 us (10%)
    all_to_all x1, waiting for transfers between devices, on_device(): lax.all_to_all(relaxed_rows, 'tm', split_axis=1, concat_axis=2, tiled=True)  47.9 us
    all_to_all x1, waiting for transfers between devices, stacked_exchange(): received = lax.all_to_all(jnp.stack(pieces), axis, 0, 0)  26.6 us
    dot_general x2, matrix products, to_space(): lax.dot_general(modal, eigenbasis, (((1,), (1,)), ((), ())), preferred_el...  20.6 us
    all_to_all x1, starting transfers between devices, stacked_exchange(): received = lax.all_to_all(jnp.stack(pieces), axis, 0, 0)  10.6 us
    unnamed x29, local copies, waits for them, and re-layouts  9.88 us
    dot_general x4, matrix products, apply_table(): jnp.einsum('kn,fnrx->fkrx', table, values.astype(jnp.float32), precision=...  8.37 us
    dot_general x1, matrix products, solve_shifted(): jnp.dot(stacked, eigenbasis, preferred_element_type=jnp.float32)  7.56 us
    squeeze x2, local copies, waits for them, and re-layouts, solve_shifted(): scaled_real = (modal[0] * shift_real + modal[1] * shift_imag) / magnitude  5.81 us
  transfers between devices with their start and end apart: 5, of which 3 were waited for; matrix products, arithmetic and copies ran while one was open for 9% of the time, Pallas kernels for 0%

profile of v1, /device:TPU:1, one launch (start us, length us, event | category | flops | bytes accessed | tf_op | source)
XLA Modules:
  0.0 197.1 jit_solution(7681795307165745848)
XLA Ops:
  0.0 5.0 %collective-permute-start.2 = (f32[4,1,64,2048]{3,2,1,0:T(8,128)}, f32[4,1,64,2048]{3,2,1,0:T(8,128)}, u32[]{:S(2)}, u32[]{:S(2)}) collective-permute-start(f32[4,1,64,2048]{3,2,1,0:T(8,128)} %param.7), channel_id=1, source_target_pairs={{0,16},{16,32},{32,48},{48,64},{64,80},{80,96},{96,112},{112,128},... | collective-permute-start | bytes 6291464 | tf_op jit(solution)/shard_map/ppermute | solution.py:34
  5.1 1.1 fusion.79
  6.1 1.3 collective-permute-start
  7.4 0.0 copy-start.4
  7.5 4.0 %collective-permute-start.1 = (f32[4,1,1,2048]{3,2,1,0:T(1,128)S(1)}, f32[4,1,1,2048]{3,2,1,0:T(1,128)S(1)}, u32[]{:S(2)}, u32[]{:S(2)}) collective-permute-start(f32[4,1,1,2048]{3,2,1,0:T(1,128)S(1)} %get-tuple-element.12), channel_id=1, source_target_pairs={{0,1},{1,2},{2,3},{3,4},{4,5},{5,6},{6,7},{7,8},{8,9},{9,10},{10,1... | collective-permute-start | bytes 98312 | tf_op jit(solution)/shard_map/ppermute | solution.py:23
  11.4 2.7 %convert_element_type.63 = bf16[4,1,64,2048]{3,2,1,0:T(8,128)(2,1)} convert(f32[4,1,64,2048]{3,2,1,0:T(8,128)} %param.7) | non-fusion elementwise | flops 524288 | bytes 3145728 | tf_op jit(solution)/shard_map/convert_element_type | solution.py:112
  14.2 0.0 copy-done.3
  14.2 0.0 copy-done.4
  14.2 0.0 copy-start.5
  14.2 0.0 copy-start.6
  14.2 0.0 copy-start
  14.3 12.0 %fusion.27 = f32[256,2048]{1,0:T(8,128)} fusion(bf16[2048,2048]{1,0:T(8,128)(2,1)} %param.9, bf16[256,2048]{1,0:T(8,128)(2,1)} %bitcast.105, f32[2048]{0:T(1024)S(1)} %copy-done.4), kind=kOutput, calls=%fused_computation.40 | convolution fusion | flops 4296015872 | bytes 11542528 | tf_op jit(solution)/shard_map/dot_general | solution.py:50
  26.3 0.0 copy-done.5
  26.3 0.0 copy-done.6
  26.3 0.2 select_reduce_fusion
  26.5 0.0 collective-permute-done
  26.6 0.0 collective-permute-done.1
  26.6 1.8 collective-permute-done.2
  28.3 3.5 %fusion.15 = bf16[4,1,64,2048]{3,2,1,0:T(8,128)(2,1)S(1)} fusion(f32[4,1,64,2048]{3,2,1,0:T(8,128)} %param.8, f32[4,1,64,2048]{3,2,1,0:T(8,128)} %collective-permute-done.2, f32[4,1,64,2048]{3,2,1,0:T(8,128)S(1)} %copy-done, f32[4,1,1,2048]{3,2,1,0:T(1,128)S(1)} %collective-permute-done.1, f32[4,1,1,2048]{3,2,1,0:T(1,128)S(1)} %collective-permute-done, ...), kind=kLoop, calls=%fused_computation.21 | loop fusion | flops 8912896 | bytes 10027028 | tf_op jit(solution)/shard_map/convert_element_type | solution.py:122
  31.9 0.6 fusion.43
  32.5 0.7 fusion.42
  33.2 0.6 fusion.41
  33.9 0.7 fusion.40
  34.5 0.6 fusion.39
  35.2 0.7 fusion.38
  35.8 0.6 fusion.37
  36.5 0.7 fusion.36
  37.1 0.6 fusion.35
  37.8 0.7 fusion.34
  38.5 0.6 fusion.33
  39.1 0.7 fusion.32
  39.8 0.6 fusion.31
  40.4 0.7 fusion.30
  41.1 0.6 fusion.29
  41.7 0.7 fusion.28
  42.4 10.6 %all-to-all-start = ((bf16[16,4,1,4,2048]{4,3,1,2,0:T(4,128)(2,1)}), bf16[16,4,1,4,2048]{4,3,1,2,0:T(4,128)(2,1)S(1)}, u32[]{:S(2)}, u32[]{:S(2)}) async-start(bf16[16,4,1,4,2048]{4,3,1,2,0:T(4,128)(2,1)} %fusion.28), calls=%async_computation | async-start | bytes 2097152 | tf_op jit(solution)/shard_map/all_to_all | solution.py:14
  53.2 0.1 broadcast_subtract_fusion
  53.3 1.2 broadcast_add_fusion
  54.5 26.6 %all-to-all-done = bf16[16,4,1,4,2048]{4,3,1,2,0:T(4,128)(2,1)S(1)} async-done(((bf16[16,4,1,4,2048]{4,3,1,2,0:T(4,128)(2,1)}), bf16[16,4,1,4,2048]{4,3,1,2,0:T(4,128)(2,1)S(1)}, u32[]{:S(2)}, u32[]{:S(2)}) %all-to-all-start) | async-done | bytes 1048608 | tf_op jit(solution)/shard_map/all_to_all | solution.py:14
  81.0 1.3 fusion.4
  82.4 1.3 fusion.5
  83.7 0.2 pad_maximum_fusion.2
  83.9 3.0 %copy.543 = bf16[8,16,4,2048]{3,2,1,0:T(4,128)(2,1)} copy(bf16[8,16,4,2048]{3,1,2,0:T(8,128)(2,1)S(1)} %pad_maximum_fusion.2) | data formatting | bytes 4194304 | tf_op jit(solution)/shard_map/concatenate | solution.py:61
  86.8 4.0 %convert_element_type.68 = bf16[512,2048]{1,0:T(8,128)(2,1)} reshape(bf16[8,16,4,2048]{3,2,1,0:T(4,128)(2,1)} %copy.543) | data formatting | bytes 4194304 | tf_op jit(solution)/shard_map/convert_element_type | solution.py:61
  90.8 7.6 %fusion.80 = f32[512,2048]{1,0:T(8,128)S(1)} fusion(bf16[512,2048]{1,0:T(8,128)(2,1)} %convert_element_type.68, bf16[2048,2048]{1,0:T(8,128)(2,1)} %param.9), kind=kOutput, calls=%fused_computation.118 | convolution fusion | flops 4294967296 | bytes 14680064 | tf_op jit(solution)/shard_map/dot_general | solution.py:63
  98.4 2.3 %fusion.77 = (f32[256,2048]{1,0:T(8,128)}, f32[256,2048]{1,0:T(8,128)}) fusion(f32[512,2048]{1,0:T(8,128)S(1)} %fusion.80), kind=kLoop, calls=%fused_computation.115 | loop fusion | bytes 8388608 | tf_op jit(solution)/shard_map/slice | solution.py:72
  100.7 2.9 %squeeze.14 = f32[4,16,4,2048]{3,2,1,0:T(4,128)} reshape(f32[256,2048]{1,0:T(8,128)} %get-tuple-element.8) | data formatting | bytes 4194304 | tf_op jit(solution)/shard_map/squeeze | solution.py:72
  103.5 2.9 %squeeze.15 = f32[4,16,4,2048]{3,2,1,0:T(4,128)} reshape(f32[256,2048]{1,0:T(8,128)} %get-tuple-element.7) | data formatting | bytes 4194304 | tf_op jit(solution)/shard_map/squeeze | solution.py:72
  106.5 0.0 copy-done.2
  106.5 3.3 %fusion.18 = (bf16[4,16,4,2048]{3,2,1,0:T(4,128)(2,1)S(1)}, bf16[4,16,4,2048]{3,2,1,0:T(4,128)(2,1)S(1)}) fusion(f32[4,16,4,2048]{3,2,1,0:T(4,128)} %squeeze.15, f32[4,16,4,2048]{3,2,1,0:T(4,128)} %squeeze.14, f32[4,16,2048]{2,1,0:T(8,128)S(1)} %copy-done.2, f32[16]{0:T(128)S(1)} %sine_multiply_fusion, f32[4,16,2048]{2,1,0:T(8,128)S(1)} %copy-done.1), kind=kLoop, calls=%fused_computation.31 | loop fusion | flops 5242880 | bytes 7340096 | tf_op jit(solution)/shard_map/convert
  109.8 2.7 %pad_maximum_fusion.3 = bf16[8,16,4,2048]{3,2,1,0:T(4,128)(2,1)} fusion(bf16[4,16,4,2048]{3,2,1,0:T(4,128)(2,1)S(1)} %get-tuple-element.6, bf16[4,16,4,2048]{3,2,1,0:T(4,128)(2,1)S(1)} %get-tuple-element.5), kind=kLoop, calls=%fused_computation.26 | loop fusion | flops 1048576 | bytes 4194304 | tf_op jit(solution)/shard_map/concatenate | solution.py:75
  112.5 4.0 %convert_element_type.70 = bf16[512,2048]{1,0:T(8,128)(2,1)} reshape(bf16[8,16,4,2048]{3,2,1,0:T(4,128)(2,1)} %pad_maximum_fusion.3) | data formatting | bytes 4194304 | tf_op jit(solution)/shard_map/convert_element_type | solution.py:76
  116.4 8.5 %convolution_convert_fusion = bf16[512,2048]{1,0:T(8,128)(2,1)S(1)} fusion(bf16[512,2048]{1,0:T(8,128)(2,1)} %convert_element_type.70, bf16[2048,2048]{1,0:T(8,128)(2,1)} %param.9), kind=kOutput, calls=%fused_computation | convolution fusion | flops 4296015872 | bytes 12582912 | tf_op jit(solution)/shard_map/dot_general | solution.py:50
  125.0 1.5 fusion.78
  126.4 1.5 squeeze.16
  127.9 2.7 %fusion.23 = f32[4,4,2048,16]{2,3,1,0:T(8,128)} fusion(bf16[4,16,4,2048]{3,2,1,0:T(4,128)(2,1)S(1)} %squeeze.16), kind=kOutput, calls=%fused_computation.36 | convolution fusion | flops 100666880 | bytes 3145728 | tf_op jit(solution)/shard_map/kn,fnrx->fkrx/dot_general | solution.py:44
  130.6 1.5 squeeze.17
  132.0 3.1 %fusion.1 = f32[4,16,4,2048]{3,1,2,0:T(8,128)S(1)} fusion(f32[4,4,2048,16]{2,3,1,0:T(8,128)} %fusion.23, bf16[4,16,4,2048]{3,2,1,0:T(4,128)(2,1)S(1)} %squeeze.17), kind=kOutput, calls=%fused_computation.5 | convolution fusion | flops 101715456 | bytes 5242880 | tf_op jit(solution)/shard_map/kn,fnrx->fkrx/dot_general | solution.py:44
  135.1 2.7 %copy.546 = f32[4,16,4,2048]{3,2,0,1:T(4,128)} copy(f32[4,16,4,2048]{3,1,2,0:T(8,128)S(1)} %fusion.1) | data formatting | bytes 4194304 | tf_op jit(solution)/shard_map/div | solution.py:131
  137.8 4.6 %all-to-all-start.1 = ((f32[4,16,4,2048]{3,2,0,1:T(4,128)}), f32[4,16,4,2048]{3,2,0,1:T(4,128)}, u32[]{:S(2)}, u32[]{:S(2)}) async-start(f32[4,16,4,2048]{3,2,0,1:T(4,128)} %copy.546), calls=%async_computation.1 | async-start | bytes 4194304 | tf_op jit(solution)/shard_map/all_to_all | solution.py:134
  142.4 47.9 %all-to-all-done.1 = f32[4,16,4,2048]{3,2,0,1:T(4,128)} async-done(((f32[4,16,4,2048]{3,2,0,1:T(4,128)}), f32[4,16,4,2048]{3,2,0,1:T(4,128)}, u32[]{:S(2)}, u32[]{:S(2)}) %all-to-all-start.1) | async-done | bytes 2097184 | tf_op jit(solution)/shard_map/all_to_all | solution.py:134
  190.3 2.8 %copy_multiply_fusion = f32[4,16,4,2048]{3,1,2,0:T(8,128)S(1)} fusion(f32[4,16,4,2048]{3,2,0,1:T(4,128)} %all-to-all-done.1, f32[]{:T(128)S(6)} %pow.8), kind=kLoop, calls=%fused_computation.28 | loop fusion | flops 524288 | bytes 4194308 | tf_op jit(solution)/shard_map/mul | solution.py:135
  193.1 1.4 copy.548
  194.5 2.6 %copy_add_fusion = f32[4,1,64,2048]{3,2,1,0:T(8,128)} fusion(f32[4,1,64,2048]{3,2,1,0:T(8,128)S(1)} %copy-done, f32[4,1,64,2048]{3,0,2,1:T(4,128)S(1)} %bitcast.103), kind=kLoop, calls=%fused_computation.27 | loop fusion | flops 524288 | bytes 6291456 | tf_op jit(solution)/shard_map/add | solution.py:135
  (10 shorter events, 0.2 us)
Async XLA Ops:
  0.0 14.2 %copy-start.3 = (s32[64,2048]{1,0:T(8,128)S(1)}, s32[64,2048]{1,0:T(8,128)}, u32[]{:S(2)}) copy-start(s32[64,2048]{1,0:T(8,128)} %param.13) | copy-start | bytes 1572868
  0.0 28.3 %collective-permute-start.2 = (f32[4,1,64,2048]{3,2,1,0:T(8,128)}, f32[4,1,64,2048]{3,2,1,0:T(8,128)}, u32[]{:S(2)}, u32[]{:S(2)}) collective-permute-start(f32[4,1,64,2048]{3,2,1,0:T(8,128)} %param.7), channel_id=1, source_target_pairs={{0,16},{16,32},{32,48},{48,64},{64,80},{80,96},{96,112},{112,128},... | collective-permute-start | bytes 6291464 | tf_op jit(solution)/shard_map/ppermute | solution.py:34
  6.1 20.4 %collective-permute-start = (f32[4,1,1,2048]{3,2,1,0:T(1,128)S(1)}, f32[4,1,1,2048]{3,2,1,0:T(1,128)S(1)}, u32[]{:S(2)}, u32[]{:S(2)}) collective-permute-start(f32[4,1,1,2048]{3,2,1,0:T(1,128)S(1)} %get-tuple-element.11), channel_id=1, source_target_pairs={{1,0},{2,1},{3,2},{4,3},{5,4},{6,5},{7,6},{8,7},{9,8},{10,9},{11,1... | collective-permute-start | bytes 98312 | tf_op jit(solution)/shard_map/ppermute | solution.py:26
  7.4 6.8 %copy-start.4 = (f32[2048]{0:T(1024)S(1)}, f32[2048]{0:T(1024)}, u32[]{:S(2)}) copy-start(f32[2048]{0:T(1024)} %param.10) | copy-start | bytes 24580
  7.5 19.1 %collective-permute-start.1 = (f32[4,1,1,2048]{3,2,1,0:T(1,128)S(1)}, f32[4,1,1,2048]{3,2,1,0:T(1,128)S(1)}, u32[]{:S(2)}, u32[]{:S(2)}) collective-permute-start(f32[4,1,1,2048]{3,2,1,0:T(1,128)S(1)} %get-tuple-element.12), channel_id=1, source_target_pairs={{0,1},{1,2},{2,3},{3,4},{4,5},{5,6},{6,7},{7,8},{8,9},{9,10},{10,1... | collective-permute-start | bytes 98312 | tf_op jit(solution)/shard_map/ppermute | solution.py:23
  14.2 12.1 %copy-start.5 = (f32[8]{0:T(128)S(1)}, f32[8]{0:T(128)}, u32[]{:S(2)}) copy-start(f32[8]{0:T(128)} %param.11) | copy-start | bytes 100
  14.2 12.1 %copy-start.6 = (s32[4]{0:T(128)S(1)}, s32[4]{0:T(128)}, u32[]{:S(2)}) copy-start(s32[4]{0:T(128)} %param.12) | copy-start | bytes 52
  14.2 14.1 %copy-start = (f32[4,1,64,2048]{3,2,1,0:T(8,128)S(1)}, f32[4,1,64,2048]{3,2,1,0:T(8,128)}, u32[]{:S(2)}) copy-start(f32[4,1,64,2048]{3,2,1,0:T(8,128)} %param.7) | copy-start | bytes 6291460
  42.4 38.6 %all-to-all-start = ((bf16[16,4,1,4,2048]{4,3,1,2,0:T(4,128)(2,1)}), bf16[16,4,1,4,2048]{4,3,1,2,0:T(4,128)(2,1)S(1)}, u32[]{:S(2)}, u32[]{:S(2)}) async-start(bf16[16,4,1,4,2048]{4,3,1,2,0:T(4,128)(2,1)} %fusion.28), calls=%async_computation | async-start | bytes 2097152 | tf_op jit(solution)/shard_map/all_to_all | solution.py:14
  103.5 3.0 %copy-start.1 = (f32[4,16,2048]{2,1,0:T(8,128)S(1)}, f32[4,16,2048]{2,1,0:T(8,128)}, u32[]{:S(2)}) copy-start(f32[4,16,2048]{2,1,0:T(8,128)} %get-tuple-element.13) | copy-start | bytes 1572868
  103.5 3.0 %copy-start.2 = (f32[4,16,2048]{2,1,0:T(8,128)S(1)}, f32[4,16,2048]{2,1,0:T(8,128)}, u32[]{:S(2)}) copy-start(f32[4,16,2048]{2,1,0:T(8,128)} %get-tuple-element.14) | copy-start | bytes 1572868
  137.8 52.5 %all-to-all-start.1 = ((f32[4,16,4,2048]{3,2,0,1:T(4,128)}), f32[4,16,4,2048]{3,2,0,1:T(4,128)}, u32[]{:S(2)}, u32[]{:S(2)}) async-start(f32[4,16,4,2048]{3,2,0,1:T(4,128)} %copy.546), calls=%async_computation.1 | async-start | bytes 4194304 | tf_op jit(solution)/shard_map/all_to_all | solution.py:134
